TPU v7x, 256 devices: a whole 4x4x8 slice. The times are simulated.
256 devices in a mesh: dp: 16 (over z, y_hi), row: 4 (over y_lo, core), col: 4 (over x).
Axes of the slice: x: 4, y: 4 (y_hi: 2, y_lo: 2; y = y_hi * 2 + y_lo), z: 8, core: 2. Of those that a mesh axis runs over, the one named last changes fastest.
Arguments:
- tokens: bfloat16 [7168, 4096], P(('dp', 'col'), 'row'), may hold values from -6 to 6
- gate_up: bfloat16 [2, 4096, 14336], P(None, 'row', ('dp', 'col')), may hold values from -0.09375 to 0.09375
- down_weight: bfloat16 [14336, 4096], P(('dp', 'col'), 'row'), may hold values from -0.046875 to 0.046875
Outputs:
- mixed: bfloat16 [7168, 4096], P(('dp', 'col'), 'row')
- col_check: float32 [4096], P('row')
- row_check: float32 [7168], P(('dp', 'col'))
All inputs are finite; a program needn't handle non-finite values.
Results may differ from a plain program's by a relative error of at most 0.0049.
Values may be sent and summed in bfloat16 or wider, within the bound.
No kernel may reach another device: no remote copies, remote signals or barrier semaphores. Data moves between devices by JAX's collectives and lax.ppermute only.
A program may use at most 128 MiB of HBM per device.

v0:
```python
import math
import jax
import jax.numpy as jnp
from jax import lax
from jax.sharding import PartitionSpec as P


def swiglu(partial_value):
    return (jax.nn.silu(partial_value[:, 0]) * partial_value[:, 1]).astype(jnp.bfloat16)


def hidden_units(partial_value):
    share = lax.psum_scatter(partial_value, "row", scatter_dimension=0, tiled=True)
    return lax.all_gather(swiglu(share), "row", axis=0, tiled=True)


def make_accumulate(hidden, shard_piece):
    columns_wide = hidden.astype(jnp.float32)
    piece_wide = shard_piece.astype(jnp.float32)
    output_part = jnp.dot(hidden, shard_piece, preferred_element_type=jnp.float32)
    column_part = jnp.dot(
        jnp.sum(columns_wide, axis=0), piece_wide, precision=lax.Precision.HIGHEST
    )
    row_part = jnp.dot(columns_wide, jnp.sum(piece_wide, axis=1), precision=lax.Precision.HIGHEST)
    return (output_part, column_part, row_part)


def per_device(tokens, gate_up, down_weight):
    total_tokens = tokens.shape[0] * lax.axis_size(("dp", "col"))
    model_width = tokens.shape[1] * lax.axis_size("row")
    group_rows = lax.all_gather(tokens, "col", axis=0, tiled=True)
    partial_value = jnp.einsum(
        "td,gdf->tgf",
        group_rows,
        lax.all_gather(gate_up, "dp", axis=2, tiled=True),
        preferred_element_type=jnp.float32,
    )
    hidden = hidden_units(partial_value)
    output_part, column_part, row_part = make_accumulate(
        hidden, lax.all_gather(down_weight, "dp", axis=0, tiled=True)
    )
    mixed, row_share = (
        lax.psum_scatter(output_part, "col", scatter_dimension=0, tiled=True),
        lax.psum_scatter(row_part, "col", scatter_dimension=0, tiled=True),
    )
    col_check = lax.psum(column_part, ("dp", "col")) / math.sqrt(total_tokens)
    row_check = lax.psum(row_share, "row") / math.sqrt(model_width)
    return (mixed.astype(jnp.bfloat16), col_check, row_check)


def solution(mesh):
    placed = (P(("dp", "col"), "row"), P(None, "row", ("dp", "col")), P(("dp", "col"), "row"))
    return jax.shard_map(
        per_device,
        mesh=mesh,
        in_specs=placed,
        out_specs=(P(("dp", "col"), "row"), P("row"), P(("dp", "col"))),
        check_vma=False,
    )
```

profile of v0, /device:TPU:8, one launch (start us, length us, event | category | flops | bytes accessed | tf_op | source)
XLA Modules:
  0.0 748.7 jit_solution(9035475301600994231)
XLA Ops:
  7.2 0.0 all-gather.4.cloned.1.call-start
  7.2 0.7 all-gather.4.cloned.1.call-update
  7.9 0.0 reduce-scatter.3.cloned.1.call-start
  7.9 14.2 %all_gather.12 = bf16[448,1024]{1,0:T(8,128)(2,1)S(1)} all-gather(bf16[112,1024]{1,0:T(8,128)(2,1)} %param.3), channel_id=1, replica_groups=mesh['dp'=16,'row'=4,'col'=4] {'col'}, dimensions={0}, use_global_device_ids=true | all-gather | bytes 1146880 | tf_op jit(solution)/shard_map/all_gather | solution.py:31
  22.2 192.1 %all-gather.4.cloned.1.call-done = bf16[2,1024,3584]{1,2,0:T(8,128)(2,1)} async-done(((bf16[2,1024,224]{1,2,0:T(8,128)(2,1)}), bf16[2,1024,3584]{1,2,0:T(8,128)(2,1)}) %all-gather.4.cloned.1.call-update) | async-done | bytes 14680080 | tf_op jit(solution)/shard_map/all_gather | solution.py:35
  214.2 22.2 %fusion.2 = f32[448,2,3584]{2,0,1:T(8,128)} fusion(bf16[2,1024,3584]{1,2,0:T(8,128)(2,1)} %all-gather.4.cloned.1.call-done, bf16[448,1024]{1,0:T(8,128)(2,1)S(1)} %all_gather.12), kind=kOutput, calls=%fused_computation.6 | convolution fusion | flops 6576668672 | bytes 28442624 | tf_op jit(solution)/shard_map/td,gdf->tgf/dot_general | solution.py:32
  236.5 0.0 reduce-scatter.3.cloned.1.call-update
  236.5 0.0 all-gather.8.cloned.1.call-start
  236.5 0.7 all-gather.8.cloned.1.call-update
  237.2 0.0 all-gather.6.cloned.1.call-start
  237.3 113.1 %reduce-scatter.3.cloned.1.call-done = f32[112,2,3584]{2,0,1:T(8,128)} async-done(((f32[448,2,3584]{2,0,1:T(8,128)}), f32[112,2,3584]{2,0,1:T(8,128)}) %reduce-scatter.3.cloned.1.call-update) | async-done | bytes 3211280 | tf_op jit(solution)/shard_map/reduce_scatter | solution.py:13
  350.3 3.2 fusion.1
  353.6 0.0 all-gather.6.cloned.1.call-update
  353.6 0.0 copy-start.1
  353.6 0.0 reduce-scatter.5.cloned.1.call-start
  353.6 126.6 %all-gather.8.cloned.1.call-done = bf16[3584,1024]{1,0:T(8,128)(2,1)} async-done(((bf16[224,1024]{1,0:T(8,128)(2,1)}), bf16[3584,1024]{1,0:T(8,128)(2,1)}) %all-gather.8.cloned.1.call-update) | async-done | bytes 7340048 | tf_op jit(solution)/shard_map/all_gather | solution.py:40
  480.3 38.6 %all-gather.6.cloned.1.call-done = bf16[448,3584]{1,0:T(8,128)(2,1)} async-done(((bf16[112,3584]{1,0:T(8,128)(2,1)}), bf16[448,3584]{1,0:T(8,128)(2,1)}) %all-gather.6.cloned.1.call-update) | async-done | bytes 3211280 | tf_op jit(solution)/shard_map/all_gather | solution.py:14
  518.8 8.8 %fusion.4 = f32[448,1024]{1,0:T(8,128)} fusion(bf16[448,3584]{1,0:T(8,128)(2,1)} %all-gather.6.cloned.1.call-done, bf16[3584,1024]{1,0:T(8,128)(2,1)} %all-gather.8.cloned.1.call-done), kind=kOutput, calls=%fused_computation.10 | convolution fusion | flops 3288334336 | bytes 12386304 | tf_op jit(solution)/shard_map/dot_general | solution.py:20
  527.6 0.0 reduce-scatter.5.cloned.1.call-update
  527.6 0.0 copy-done.1
  527.6 0.6 dynamic-slice
  528.9 0.0 copy-start
  528.9 4.3 convert_reduce_fusion
  533.2 0.0 copy-done
  533.2 0.6 convert_reduce_fusion.1
  533.8 2.6 fusion.6
  536.4 10.9 %all-reduce = f32[448]{0:T(512)S(1)} all-reduce(f32[448]{0:T(512)S(1)} %bitcast.24), channel_id=4, replica_groups=mesh['dp'=16,'row'=4,'col'=4] {'col'}, use_global_device_ids=true, to_apply=%region_5.6.clone | all-reduce | flops 448 | bytes 3584
  547.2 0.1 dynamic-slice.1
  547.3 6.5 psum.15
  553.8 5.2 fusion.5
  559.0 180.3 %psum.14 = f32[1024]{0:T(1024)S(1)} all-reduce(f32[1024]{0:T(1024)S(1)} %bitcast.23), channel_id=1, replica_groups=mesh['dp'=16,'row'=4,'col'=4] {'dp','col'}, use_global_device_ids=true, to_apply=%region_3.4 | all-reduce | flops 1024 | bytes 8192 | tf_op jit(solution)/shard_map/psum | solution.py:46
  739.3 0.5 broadcast_multiply_fusion.1
  739.8 0.6 broadcast_multiply_fusion
  740.4 0.0 reduce-scatter.5.cloned.1.call-done
  740.4 1.7 convert_element_type.13
  (2 shorter events, 0.0 us)
Async XLA Ops:
  7.2 207.1 %all-gather.4.cloned.1.call-start = ((), (), s32[]{:S(2)}) async-start(), calls=%async_computation.2 | async-start | bytes 15597568 | tf_op jit(solution)/shard_map/all_gather | solution.py:35
  7.9 342.4 %reduce-scatter.3.cloned.1.call-start = ((), (), s32[]{:S(2)}) async-start(), calls=%async_computation.3 | async-start | bytes 16056320 | tf_op jit(solution)/shard_map/reduce_scatter | solution.py:13
  236.5 243.8 %all-gather.8.cloned.1.call-start = ((), (), s32[]{:S(2)}) async-start(), calls=%async_computation.5 | async-start | bytes 7798784 | tf_op jit(solution)/shard_map/all_gather | solution.py:40
  237.2 281.6 %all-gather.6.cloned.1.call-start = ((), (), s32[]{:S(2)}) async-start(), calls=%async_computation.4 | async-start | bytes 4014080 | tf_op jit(solution)/shard_map/all_gather | solution.py:14
  353.6 174.1 %copy-start.1 = (u32[256]{0:T(256)S(1)}, u32[256]{0:T(256)}, u32[]{:S(2)}) copy-start(u32[256]{0:T(256)} %constant.16) | copy-start | bytes 3076
  353.6 386.8 %reduce-scatter.5.cloned.1.call-start = ((), (), s32[]{:S(2)}) async-start(), calls=%async_computation.6 | async-start | bytes 2293760 | tf_op jit(solution)/shard_map/reduce_scatter | solution.py:43
  528.9 4.3 copy-start
Sparse Core Ops, SparseCore 0:
  10.6 203.5 all-gather.3
  236.6 113.6 reduce-scatter.2
  352.9 127.3 all-gather.7
  481.9 36.8 all-gather.5
  527.7 32.7 reduce-scatter.4
where the time goes:
time: 749 us
  waiting for transfers between devices  472 us (63%)
  blocking collectives  212 us (28%)
  matrix products  38.7 us (5%)
  between operations  14.5 us (2%)
  other arithmetic  10.9 us (1%)
    all_gather x1, waiting for transfers between devices, per_device(): lax.all_gather(gate_up, 'dp', axis=2, tiled=True)  192 us
    psum x1, blocking collectives, per_device(): col_check = lax.psum(column_part, ('dp', 'col')) / math.sqrt(total_tokens)  180 us
    all_gather x1, waiting for transfers between devices, per_device(): lax.all_gather(down_weight, 'dp', axis=0, tiled=True)  127 us
    reduce_scatter x1, waiting for transfers between devices, hidden_units(): lax.psum_scatter(partial_value, 'row', scatter_dimension=0, tiled=True)  113 us
    all_gather x1, waiting for transfers between devices, hidden_units(): return lax.all_gather(swiglu(share), 'row', axis=0, tiled=True)  38.6 us
    dot_general x1, matrix products, per_device(): jnp.einsum('td,gdf->tgf', group_rows, lax.all_gather(gate_up, 'dp', axis=...  22.2 us
  transfers between devices with their start and end apart: 5, of which 4 were waited for; matrix products, arithmetic and copies ran while one was open for 2% of the time, Pallas kernels for 0%

commit v1 on v0

--- a/solution.py
+++ b/solution.py
@@ -1,8 +1,18 @@
+import functools
 import math
 import jax
 import jax.numpy as jnp
 from jax import lax
 from jax.sharding import PartitionSpec as P
+
+
+def feed_series(buf, along_axis, device_axis):
+    for u in (along_axis, device_axis):
+        buf = lax.psum(buf, axis_name=u)
+    return buf
+
+
+deliver_strips_all = functools.partial(feed_series, along_axis="dp", device_axis="col")
 
 
 def swiglu(partial_value):
@@ -43,7 +53,7 @@
         lax.psum_scatter(output_part, "col", scatter_dimension=0, tiled=True),
         lax.psum_scatter(row_part, "col", scatter_dimension=0, tiled=True),
     )
-    col_check = lax.psum(column_part, ("dp", "col")) / math.sqrt(total_tokens)
+    col_check = deliver_strips_all(column_part) / math.sqrt(total_tokens)
     row_check = lax.psum(row_share, "row") / math.sqrt(model_width)
     return (mixed.astype(jnp.bfloat16), col_check, row_check)
 

time: 749 us -> 610 us (0.81)
  blocking collectives: 212 us -> 72.6 us
    psum x1 -> x2, blocking collectives: 180 us -> 52.7 us  [feed_series(): buf = lax.psum(buf, axis_name=u)]
    unnamed x1 -> x0, blocking collectives: 10.9 us -> none
  transfers between devices with their start and end apart: 5 -> 5, of which waited for: 4 -> 4; matrix products, arithmetic and copies ran while one was open for 2% -> 3% of each run, Pallas kernels for 0% -> 0%
where the time goes in v1:
time: 610 us; the launch traced here: 608 us
  waiting for transfers between devices  472 us (77%)
  blocking collectives  72.6 us (12%)
  matrix products  36.5 us (6%)
  between operations  14.8 us (2%)
  other arithmetic  10.9 us (2%)
    all_gather x1, waiting for transfers between devices, per_device(): lax.all_gather(gate_up, 'dp', axis=2, tiled=True)  192 us
    all_gather x1, waiting for transfers between devices, per_device(): lax.all_gather(down_weight, 'dp', axis=0, tiled=True)  127 us
    reduce_scatter x1, waiting for transfers between devices, hidden_units(): lax.psum_scatter(partial_value, 'row', scatter_dimension=0, tiled=True)  113 us
    psum x2, blocking collectives, feed_series(): buf = lax.psum(buf, axis_name=u)  52.7 us
    all_gather x1, waiting for transfers between devices, hidden_units(): return lax.all_gather(swiglu(share), 'row', axis=0, tiled=True)  38.6 us
    dot_general x1, matrix products, per_device(): jnp.einsum('td,gdf->tgf', group_rows, lax.all_gather(gate_up, 'dp', axis=...  22.2 us
    all_gather x1, blocking collectives, per_device(): group_rows = lax.all_gather(tokens, 'col', axis=0, tiled=True)  14.2 us
  transfers between devices with their start and end apart: 5, of which 4 were waited for; matrix products, arithmetic and copies ran while one was open for 3% of the time, Pallas kernels for 0%

profile of v1, /device:TPU:8, one launch (start us, length us, event | category | flops | bytes accessed | tf_op | source)
XLA Modules:
  0.0 607.8 jit_solution(11758015143369375772)
XLA Ops:
  7.2 0.0 all-gather.4.cloned.1.call-start
  7.2 0.7 all-gather.4.cloned.1.call-update
  7.9 0.0 reduce-scatter.3.cloned.1.call-start
  7.9 14.2 %all_gather.12 = bf16[448,1024]{1,0:T(8,128)(2,1)S(1)} all-gather(bf16[112,1024]{1,0:T(8,128)(2,1)} %param.3), channel_id=1, replica_groups=mesh['dp'=16,'row'=4,'col'=4] {'col'}, dimensions={0}, use_global_device_ids=true | all-gather | bytes 1146880 | tf_op jit(solution)/shard_map/all_gather | solution.py:41
  22.2 192.1 %all-gather.4.cloned.1.call-done = bf16[2,1024,3584]{1,2,0:T(8,128)(2,1)} async-done(((bf16[2,1024,224]{1,2,0:T(8,128)(2,1)}), bf16[2,1024,3584]{1,2,0:T(8,128)(2,1)}) %all-gather.4.cloned.1.call-update) | async-done | bytes 14680080 | tf_op jit(solution)/shard_map/all_gather | solution.py:45
  214.2 22.2 %fusion.2 = f32[448,2,3584]{2,0,1:T(8,128)} fusion(bf16[2,1024,3584]{1,2,0:T(8,128)(2,1)} %all-gather.4.cloned.1.call-done, bf16[448,1024]{1,0:T(8,128)(2,1)S(1)} %all_gather.12), kind=kOutput, calls=%fused_computation.6 | convolution fusion | flops 6576668672 | bytes 28442624 | tf_op jit(solution)/shard_map/td,gdf->tgf/dot_general | solution.py:42
  236.5 0.0 reduce-scatter.3.cloned.1.call-update
  236.5 0.0 all-gather.8.cloned.1.call-start
  236.5 0.7 all-gather.8.cloned.1.call-update
  237.2 0.0 all-gather.6.cloned.1.call-start
  237.3 113.1 %reduce-scatter.3.cloned.1.call-done = f32[112,2,3584]{2,0,1:T(8,128)} async-done(((f32[448,2,3584]{2,0,1:T(8,128)}), f32[112,2,3584]{2,0,1:T(8,128)}) %reduce-scatter.3.cloned.1.call-update) | async-done | bytes 3211280 | tf_op jit(solution)/shard_map/reduce_scatter | solution.py:23
  350.3 3.2 fusion.1
  353.6 0.0 all-gather.6.cloned.1.call-update
  353.6 0.0 copy-start.2
  353.6 0.0 reduce-scatter.5.cloned.1.call-start
  353.6 126.6 %all-gather.8.cloned.1.call-done = bf16[3584,1024]{1,0:T(8,128)(2,1)} async-done(((bf16[224,1024]{1,0:T(8,128)(2,1)}), bf16[3584,1024]{1,0:T(8,128)(2,1)}) %all-gather.8.cloned.1.call-update) | async-done | bytes 7340048 | tf_op jit(solution)/shard_map/all_gather | solution.py:50
  480.3 38.6 %all-gather.6.cloned.1.call-done = bf16[448,3584]{1,0:T(8,128)(2,1)} async-done(((bf16[112,3584]{1,0:T(8,128)(2,1)}), bf16[448,3584]{1,0:T(8,128)(2,1)}) %all-gather.6.cloned.1.call-update) | async-done | bytes 3211280 | tf_op jit(solution)/shard_map/all_gather | solution.py:24
  518.8 8.8 %fusion.4 = f32[448,1024]{1,0:T(8,128)} fusion(bf16[448,3584]{1,0:T(8,128)(2,1)} %all-gather.6.cloned.1.call-done, bf16[3584,1024]{1,0:T(8,128)(2,1)} %all-gather.8.cloned.1.call-done), kind=kOutput, calls=%fused_computation.10 | convolution fusion | flops 3288334336 | bytes 12386304 | tf_op jit(solution)/shard_map/dot_general | solution.py:30
  527.6 0.0 copy-start.1
  527.6 0.0 reduce-scatter.5.cloned.1.call-update
  527.6 0.0 copy-done.2
  527.6 0.6 dynamic-slice
  529.2 0.0 copy-start
  529.2 4.3 convert_reduce_fusion
  533.5 0.0 copy-done.1
  533.5 0.6 convert_reduce_fusion.1
  534.1 0.3 copy-done
  534.4 2.9 fusion.5
  537.4 42.2 %psum.21 = f32[1024]{0:T(1024)S(1)} all-reduce(f32[1024]{0:T(1024)S(1)} %bitcast.23), channel_id=1, replica_groups=mesh['dp'=16,'row'=4,'col'=4] {'dp'}, use_global_device_ids=true, to_apply=%region_3.4 | all-reduce | flops 1024 | bytes 8192 | tf_op jit(solution)/shard_map/psum | solution.py:11
  579.6 2.6 fusion.6
  582.1 10.5 %all-reduce.1 = (f32[1024]{0:T(1024)S(1)}, f32[448]{0:T(512)S(1)}) all-reduce(f32[1024]{0:T(1024)S(1)} %psum.21, f32[448]{0:T(512)S(1)} %bitcast.24), channel_id=1, replica_groups=mesh['dp'=16,'row'=4,'col'=4] {'col'}, use_global_device_ids=true, to_apply=%region_4.5 | all-reduce | flops 1472 | bytes 11776 | tf_op jit(solution)/shard_map/psum | solution.py:11
  592.7 0.1 dynamic-slice.1
  592.7 5.6 psum.23
  598.4 0.5 broadcast_multiply_fusion.1
  598.9 0.6 broadcast_multiply_fusion
  599.5 0.0 reduce-scatter.5.cloned.1.call-done
  599.5 1.7 convert_element_type.13
  (2 shorter events, 0.0 us)
Async XLA Ops:
  7.2 207.1 %all-gather.4.cloned.1.call-start = ((), (), s32[]{:S(2)}) async-start(), calls=%async_computation.2 | async-start | bytes 15597568 | tf_op jit(solution)/shard_map/all_gather | solution.py:45
  7.9 342.4 %reduce-scatter.3.cloned.1.call-start = ((), (), s32[]{:S(2)}) async-start(), calls=%async_computation.3 | async-start | bytes 16056320 | tf_op jit(solution)/shard_map/reduce_scatter | solution.py:23
  236.5 243.8 %all-gather.8.cloned.1.call-start = ((), (), s32[]{:S(2)}) async-start(), calls=%async_computation.5 | async-start | bytes 7798784 | tf_op jit(solution)/shard_map/all_gather | solution.py:50
  237.2 281.6 %all-gather.6.cloned.1.call-start = ((), (), s32[]{:S(2)}) async-start(), calls=%async_computation.4 | async-start | bytes 4014080 | tf_op jit(solution)/shard_map/all_gather | solution.py:24
  353.6 174.1 %copy-start.2 = (u32[256]{0:T(256)S(1)}, u32[256]{0:T(256)}, u32[]{:S(2)}) copy-start(u32[256]{0:T(256)} %constant.16) | copy-start | bytes 3076
  353.6 245.9 %reduce-scatter.5.cloned.1.call-start = ((), (), s32[]{:S(2)}) async-start(), calls=%async_computation.6 | async-start | bytes 2293760 | tf_op jit(solution)/shard_map/reduce_scatter | solution.py:53
  527.6 5.9 copy-start.1
  529.2 5.3 copy-start
Sparse Core Ops, SparseCore 0:
  10.6 203.5 all-gather.3
  236.6 113.6 reduce-scatter.2
  352.9 127.3 all-gather.7
  481.9 36.8 all-gather.5
  527.7 32.6 reduce-scatter.4
